TPU v7x, 512 devices: a whole 4x8x8 slice. The times are simulated.
512 devices in a mesh: lat: 16 (over x_hi, y), lon: 32 (over z, x_lo, core).
Axes of the slice: x: 4 (x_hi: 2, x_lo: 2; x = x_hi * 2 + x_lo), y: 8, z: 8, core: 2. Of those that a mesh axis runs over, the one named last changes fastest.
Arguments:
- height: float32 [1024, 8640], P('lat', 'lon'), may hold values from -6 to 6
- east_flow: float32 [1024, 8640], P('lat', 'lon'), may hold values from -4 to 4
- north_flow: float32 [1024, 8640], P('lat', 'lon'), may hold values from -4 to 4
- legendre: float32 [128, 1024, 2048], P('lon', 'lat'), may hold values from -0.1875 to 0.1875
- love_numbers: float32 [2048], replicated, may hold values from 0.05 to 1
- wavenumbers: int32 [128], replicated, may hold values from 0 to 2047, as said below
- land_sea: int32 [1024, 8640], P('lat', 'lon'), may hold values 0 or 1
Outputs:
- loading: float32 [1024, 8640], P('lat', 'lon')
- surface: float32 [1024, 8640], P('lat', 'lon')
- east_out: float32 [1024, 8640], P('lat', 'lon')
- north_out: float32 [1024, 8640], P('lat', 'lon')
Inputs may be any that keep to these rules, and one draw needn't show every extreme that they name: 128 distinct wavenumbers in no particular order; 0 and 2047 are always among them.
All inputs are finite; a program needn't handle non-finite values. No bound on the sum of `land_sea` on one device may be relied on, other than what follows from the above.
Results may differ from a plain program's by a relative error of at most 0.000078.
Values sent between devices are 32-bit elements; how exact they have to be, the bound alone decides.
A program may use at most 64 MiB of HBM per device.

v0:
```python
import math
import jax
import jax.numpy as jnp
from jax import lax
from jax.sharding import PartitionSpec as P

SUBSTEPS = 4
east_step = 0.3
north_step = 0.3


def extended(block, sides, width, periodic):
    for axis, dim in sides:
        count = lax.axis_size(axis)
        forward = [(i, i + 1) for i in range(count - 1)]
        if periodic:
            forward.append((count - 1, 0))
        backward = [(target, source) for source, target in forward]
        low = lax.ppermute(
            lax.slice_in_dim(block, block.shape[dim] - width, None, axis=dim), axis, forward
        )
        high = lax.ppermute(lax.slice_in_dim(block, 0, width, axis=dim), axis, backward)
        block = jnp.concatenate([low, block, high], axis=dim)
    return block


def harmonic_rows(wavenumbers, first_column, column_count, period):
    columns = first_column + jnp.arange(column_count, dtype=jnp.int32)
    product = wavenumbers[:, None] * columns[None, :] % period
    angles = 2.0 * math.pi / period * product.astype(jnp.float32)
    stacked = jnp.stack([jnp.cos(angles), jnp.sin(angles)], axis=1)
    return stacked.reshape(2 * wavenumbers.shape[0], column_count)


def band_rim(field):
    return extended(field, (("lat", 0),), 1, False)


def sector_rim(field):
    return extended(field, (("lon", 1),), 1, True)


def shards(height, east_flow, north_flow, legendre, love_numbers, wavenumbers, land_sea):
    highest = lax.Precision.HIGHEST
    band_rows, sector_cols = height.shape
    all_cols = sector_cols * lax.axis_size("lon")
    all_waves = wavenumbers.shape[0]
    own_waves = legendre.shape[0]
    sector_index = lax.axis_index("lon")
    harmonics = harmonic_rows(wavenumbers, sector_index * sector_cols, sector_cols, all_cols)
    forward_scale = 1.0 / math.sqrt(all_cols)
    partial_rows = forward_scale * lax.dot_general(
        harmonics, height, (((1,), (1,)), ((), ())), precision=highest
    )
    totals = lax.psum(partial_rows, "lon")
    owned = lax.dynamic_slice_in_dim(totals, sector_index * (2 * own_waves), 2 * own_waves, 0)
    owned = owned.reshape(own_waves, 2, band_rows)
    partial_value = jnp.einsum("mtl,mpt->mpl", legendre, owned, precision=highest)
    spectral = lax.psum(partial_value, "lat") * love_numbers[None, None, :]
    synthesized = jnp.einsum("mtl,mpl->mpt", legendre, spectral, precision=highest).reshape(
        2 * own_waves, band_rows
    )
    back_scale = 1.0 / math.sqrt(all_waves)
    loading = (
        lax.dot_general(
            lax.all_gather(synthesized, "lon", axis=0, tiled=True),
            harmonics,
            (((0,), (0,)), ((), ())),
            precision=highest,
        )
        * back_scale
    )
    wet_cells = land_sea.astype(jnp.float32)
    surface = height
    east_out = east_flow
    north_out = north_flow
    for substep in range(SUBSTEPS):
        pressure = surface - loading
        pressure_lat = band_rim(pressure)
        pressure_lon = sector_rim(pressure)
        east_out = wet_cells * (east_out - east_step * (pressure_lon[:, 2:] - pressure_lon[:, :-2]))
        north_out = wet_cells * (north_out - north_step * (pressure_lat[2:] - pressure_lat[:-2]))
        east_wide = sector_rim(east_out)
        north_wide = band_rim(north_out)
        change = east_step * (east_wide[:, 2:] - east_wide[:, :-2]) + north_step * (
            north_wide[2:] - north_wide[:-2]
        )
        surface = surface - wet_cells * change
    return (loading, surface, east_out, north_out)


def solution(mesh):
    return jax.shard_map(
        shards,
        mesh=mesh,
        in_specs=(
            P("lat", "lon"),
            P("lat", "lon"),
            P("lat", "lon"),
            P("lon", "lat", None),
            P(),
            P(),
            P("lat", "lon"),
        ),
        out_specs=(P("lat", "lon"), P("lat", "lon"), P("lat", "lon"), P("lat", "lon")),
        check_vma=False,
    )
```

profile of v0, /device:TPU:56, one launch (start us, length us, event | category | flops | bytes accessed | tf_op | source)
XLA Modules:
  0.0 582.8 jit_solution(6953861917037026702)
XLA Ops:
  7.2 7.9 %fusion.62 = (f32[128,1,270]{2,1,0:T(1,128)S(1)}, f32[128,1,270]{2,1,0:T(1,128)S(1)}) fusion(s32[270]{0:T(512)S(1)} %iota_add_fusion, s32[128]{0:T(128)} %param.12), kind=kLoop, calls=%fused_computation.98 | loop fusion | flops 311040 | bytes 278072 | tf_op jit(solution)/shard_map/cos | solution.py:31
  15.9 2.0 convolution_multiply_fusion
  18.0 215.3 %all-reduce.3.cloned.1.call-done = f32[256,64]{1,0:T(8,128)} async-done(((f32[256,64]{1,0:T(8,128)}), f32[256,64]{1,0:T(8,128)}) %all-reduce.3.cloned.1.call-update) | async-done | bytes 65552 | tf_op jit(solution)/shard_map/psum | solution.py:55
  235.7 149.2 %all-reduce.5.cloned.1.call-done = f32[4,2,2048]{2,1,0:T(2,128)} async-done(((f32[4,2,2048]{2,1,0:T(2,128)}), f32[4,2,2048]{2,1,0:T(2,128)}) %all-reduce.5.cloned.1.call-update) | async-done | bytes 65552 | tf_op jit(solution)/shard_map/psum | solution.py:59
  384.8 2.7 fusion.58
  387.5 35.5 %all_gather.3 = f32[256,64]{1,0:T(8,128)S(1)} all-gather(f32[8,64]{1,0:T(8,128)S(1)} %bitcast.9), channel_id=1, replica_groups=mesh['lat'=16,'lon'=32] {'lon'}, dimensions={0}, use_global_device_ids=true | all-gather | bytes 67584 | tf_op jit(solution)/shard_map/all_gather | solution.py:66
  423.5 1.9 collective-permute-start.4
  425.4 7.5 %collective-permute-start.5 = (f32[1,270]{1,0:T(1,128)S(1)}, f32[1,270]{1,0:T(1,128)S(1)}, u32[]{:S(2)}, u32[]{:S(2)}) collective-permute-start(f32[1,270]{1,0:T(1,128)S(1)} %get-tuple-element.49), channel_id=1, source_target_pairs={{0,32},{32,64},{64,96},{96,128},{128,160},{160,192},{192,224},{224... | collective-permute-start | bytes 3248 | tf_op jit(solution)/shard_map/ppermute | solution.py:19
  435.0 2.4 collective-permute-start.1
  437.4 4.9 collective-permute-done.1
  442.5 1.9 collective-permute-start.6
  444.4 7.5 %collective-permute-start.7 = (f32[1,270]{1,0:T(1,128)S(1)}, f32[1,270]{1,0:T(1,128)S(1)}, u32[]{:S(2)}, u32[]{:S(2)}) collective-permute-start(f32[1,270]{1,0:T(1,128)S(1)} %get-tuple-element.47), channel_id=1, source_target_pairs={{0,32},{32,64},{64,96},{96,128},{128,160},{160,192},{192,224},{224... | collective-permute-start | bytes 3248 | tf_op jit(solution)/shard_map/ppermute | solution.py:19
  454.0 2.4 collective-permute-start.3
  456.4 4.9 collective-permute-done.3
  463.4 7.5 %collective-permute-start.13 = (f32[1,270]{1,0:T(1,128)S(1)}, f32[1,270]{1,0:T(1,128)S(1)}, u32[]{:S(2)}, u32[]{:S(2)}) collective-permute-start(f32[1,270]{1,0:T(1,128)S(1)} %get-tuple-element.41), channel_id=1, source_target_pairs={{0,32},{32,64},{64,96},{96,128},{128,160},{160,192},{192,224},{224... | collective-permute-start | bytes 3248 | tf_op jit(solution)/shard_map/ppermute | solution.py:19
  472.9 2.4 collective-permute-start.9
  475.4 4.9 collective-permute-done.9
  482.4 7.5 %collective-permute-start.15 = (f32[1,270]{1,0:T(1,128)S(1)}, f32[1,270]{1,0:T(1,128)S(1)}, u32[]{:S(2)}, u32[]{:S(2)}) collective-permute-start(f32[1,270]{1,0:T(1,128)S(1)} %get-tuple-element.39), channel_id=1, source_target_pairs={{0,32},{32,64},{64,96},{96,128},{128,160},{160,192},{192,224},{224... | collective-permute-start | bytes 3248 | tf_op jit(solution)/shard_map/ppermute | solution.py:19
  491.9 2.4 collective-permute-start.11
  494.3 4.9 collective-permute-done.11
  501.3 7.5 %collective-permute-start.21 = (f32[1,270]{1,0:T(1,128)S(1)}, f32[1,270]{1,0:T(1,128)S(1)}, u32[]{:S(2)}, u32[]{:S(2)}) collective-permute-start(f32[1,270]{1,0:T(1,128)S(1)} %get-tuple-element.33), channel_id=1, source_target_pairs={{0,32},{32,64},{64,96},{96,128},{128,160},{160,192},{192,224},{224... | collective-permute-start | bytes 3248 | tf_op jit(solution)/shard_map/ppermute | solution.py:19
  510.9 2.4 collective-permute-start.17
  513.3 4.9 collective-permute-done.17
  520.3 7.5 %collective-permute-start.23 = (f32[1,270]{1,0:T(1,128)S(1)}, f32[1,270]{1,0:T(1,128)S(1)}, u32[]{:S(2)}, u32[]{:S(2)}) collective-permute-start(f32[1,270]{1,0:T(1,128)S(1)} %get-tuple-element.31), channel_id=1, source_target_pairs={{0,32},{32,64},{64,96},{96,128},{128,160},{160,192},{192,224},{224... | collective-permute-start | bytes 3248 | tf_op jit(solution)/shard_map/ppermute | solution.py:19
  529.9 2.4 collective-permute-start.19
  532.3 4.9 collective-permute-done.19
  539.3 7.5 %collective-permute-start.29 = (f32[1,270]{1,0:T(1,128)S(1)}, f32[1,270]{1,0:T(1,128)S(1)}, u32[]{:S(2)}, u32[]{:S(2)}) collective-permute-start(f32[1,270]{1,0:T(1,128)S(1)} %get-tuple-element.25), channel_id=1, source_target_pairs={{0,32},{32,64},{64,96},{96,128},{128,160},{160,192},{192,224},{224... | collective-permute-start | bytes 3248 | tf_op jit(solution)/shard_map/ppermute | solution.py:19
  548.8 2.4 collective-permute-start.25
  551.3 4.9 collective-permute-done.25
  558.3 7.5 %collective-permute-start.31 = (f32[1,270]{1,0:T(1,128)S(1)}, f32[1,270]{1,0:T(1,128)S(1)}, u32[]{:S(2)}, u32[]{:S(2)}) collective-permute-start(f32[1,270]{1,0:T(1,128)S(1)} %get-tuple-element.23), channel_id=1, source_target_pairs={{0,32},{32,64},{64,96},{96,128},{128,160},{160,192},{192,224},{224... | collective-permute-start | bytes 3248 | tf_op jit(solution)/shard_map/ppermute | solution.py:19
  567.8 2.4 collective-permute-start.27
  570.3 4.9 collective-permute-done.27
  (90 shorter events, 32.9 us)
Async XLA Ops:
  7.2 226.1 %all-reduce.3.cloned.1.call-start = ((), (), s32[]{:S(2)}) async-start(), calls=%async_computation | async-start | bytes 262144 | tf_op jit(solution)/shard_map/psum | solution.py:55
  17.9 366.9 %all-reduce.5.cloned.1.call-start = ((), (), s32[]{:S(2)}) async-start(), calls=%async_computation.1 | async-start | bytes 131072 | tf_op jit(solution)/shard_map/psum | solution.py:59
  423.5 18.8 %collective-permute-start.4 = (f32[1,270]{1,0:T(1,128)S(1)}, f32[1,270]{1,0:T(1,128)S(1)}, u32[]{:S(2)}, u32[]{:S(2)}) collective-permute-start(f32[1,270]{1,0:T(1,128)S(1)} %get-tuple-element.48), channel_id=1, source_target_pairs={{32,0},{64,32},{96,64},{128,96},{160,128},{192,160},{224,192},{256... | collective-permute-start | bytes 3248 | tf_op jit(solution)/shard_map/ppermute | solution.py:22
  425.4 16.9 %collective-permute-start.5 = (f32[1,270]{1,0:T(1,128)S(1)}, f32[1,270]{1,0:T(1,128)S(1)}, u32[]{:S(2)}, u32[]{:S(2)}) collective-permute-start(f32[1,270]{1,0:T(1,128)S(1)} %get-tuple-element.49), channel_id=1, source_target_pairs={{0,32},{32,64},{64,96},{96,128},{128,160},{160,192},{192,224},{224... | collective-permute-start | bytes 3248 | tf_op jit(solution)/shard_map/ppermute | solution.py:19
  433.0 4.3 collective-permute-start
  435.0 7.3 %collective-permute-start.1 = (f32[64,1]{1,0:T(8,128)S(1)}, f32[64,1]{1,0:T(8,128)S(1)}, u32[]{:S(2)}, u32[]{:S(2)}) collective-permute-start(f32[64,1]{1,0:T(8,128)S(1)} %get-tuple-element.45), channel_id=1, source_target_pairs={{0,1},{1,2},{2,3},{3,4},{4,5},{5,6},{6,7},{7,8},{8,9},{9,10},{10,1... | collective-permute-start | bytes 776 | tf_op jit(solution)/shard_map/ppermute | solution.py:19
  442.5 18.8 %collective-permute-start.6 = (f32[1,270]{1,0:T(1,128)S(1)}, f32[1,270]{1,0:T(1,128)S(1)}, u32[]{:S(2)}, u32[]{:S(2)}) collective-permute-start(f32[1,270]{1,0:T(1,128)S(1)} %get-tuple-element.46), channel_id=1, source_target_pairs={{32,0},{64,32},{96,64},{128,96},{160,128},{192,160},{224,192},{256... | collective-permute-start | bytes 3248 | tf_op jit(solution)/shard_map/ppermute | solution.py:22
  444.4 16.9 %collective-permute-start.7 = (f32[1,270]{1,0:T(1,128)S(1)}, f32[1,270]{1,0:T(1,128)S(1)}, u32[]{:S(2)}, u32[]{:S(2)}) collective-permute-start(f32[1,270]{1,0:T(1,128)S(1)} %get-tuple-element.47), channel_id=1, source_target_pairs={{0,32},{32,64},{64,96},{96,128},{128,160},{160,192},{192,224},{224... | collective-permute-start | bytes 3248 | tf_op jit(solution)/shard_map/ppermute | solution.py:19
  452.0 4.3 collective-permute-start.2
  454.0 7.3 %collective-permute-start.3 = (f32[64,1]{1,0:T(8,128)S(1)}, f32[64,1]{1,0:T(8,128)S(1)}, u32[]{:S(2)}, u32[]{:S(2)}) collective-permute-start(f32[64,1]{1,0:T(8,128)S(1)} %get-tuple-element.43), channel_id=1, source_target_pairs={{0,1},{1,2},{2,3},{3,4},{4,5},{5,6},{6,7},{7,8},{8,9},{9,10},{10,1... | collective-permute-start | bytes 776 | tf_op jit(solution)/shard_map/ppermute | solution.py:19
  461.5 18.8 %collective-permute-start.12 = (f32[1,270]{1,0:T(1,128)S(1)}, f32[1,270]{1,0:T(1,128)S(1)}, u32[]{:S(2)}, u32[]{:S(2)}) collective-permute-start(f32[1,270]{1,0:T(1,128)S(1)} %get-tuple-element.40), channel_id=1, source_target_pairs={{32,0},{64,32},{96,64},{128,96},{160,128},{192,160},{224,192},{256... | collective-permute-start | bytes 3248 | tf_op jit(solution)/shard_map/ppermute | solution.py:22
  463.4 16.9 %collective-permute-start.13 = (f32[1,270]{1,0:T(1,128)S(1)}, f32[1,270]{1,0:T(1,128)S(1)}, u32[]{:S(2)}, u32[]{:S(2)}) collective-permute-start(f32[1,270]{1,0:T(1,128)S(1)} %get-tuple-element.41), channel_id=1, source_target_pairs={{0,32},{32,64},{64,96},{96,128},{128,160},{160,192},{192,224},{224... | collective-permute-start | bytes 3248 | tf_op jit(solution)/shard_map/ppermute | solution.py:19
  471.0 4.3 collective-permute-start.8
  472.9 7.3 %collective-permute-start.9 = (f32[64,1]{1,0:T(8,128)S(1)}, f32[64,1]{1,0:T(8,128)S(1)}, u32[]{:S(2)}, u32[]{:S(2)}) collective-permute-start(f32[64,1]{1,0:T(8,128)S(1)} %get-tuple-element.37), channel_id=1, source_target_pairs={{0,1},{1,2},{2,3},{3,4},{4,5},{5,6},{6,7},{7,8},{8,9},{9,10},{10,1... | collective-permute-start | bytes 776 | tf_op jit(solution)/shard_map/ppermute | solution.py:19
  480.4 18.8 %collective-permute-start.14 = (f32[1,270]{1,0:T(1,128)S(1)}, f32[1,270]{1,0:T(1,128)S(1)}, u32[]{:S(2)}, u32[]{:S(2)}) collective-permute-start(f32[1,270]{1,0:T(1,128)S(1)} %get-tuple-element.38), channel_id=1, source_target_pairs={{32,0},{64,32},{96,64},{128,96},{160,128},{192,160},{224,192},{256... | collective-permute-start | bytes 3248 | tf_op jit(solution)/shard_map/ppermute | solution.py:22
  482.4 16.9 %collective-permute-start.15 = (f32[1,270]{1,0:T(1,128)S(1)}, f32[1,270]{1,0:T(1,128)S(1)}, u32[]{:S(2)}, u32[]{:S(2)}) collective-permute-start(f32[1,270]{1,0:T(1,128)S(1)} %get-tuple-element.39), channel_id=1, source_target_pairs={{0,32},{32,64},{64,96},{96,128},{128,160},{160,192},{192,224},{224... | collective-permute-start | bytes 3248 | tf_op jit(solution)/shard_map/ppermute | solution.py:19
  490.0 4.3 collective-permute-start.10
  491.9 7.3 %collective-permute-start.11 = (f32[64,1]{1,0:T(8,128)S(1)}, f32[64,1]{1,0:T(8,128)S(1)}, u32[]{:S(2)}, u32[]{:S(2)}) collective-permute-start(f32[64,1]{1,0:T(8,128)S(1)} %get-tuple-element.35), channel_id=1, source_target_pairs={{0,1},{1,2},{2,3},{3,4},{4,5},{5,6},{6,7},{7,8},{8,9},{9,10},{10,1... | collective-permute-start | bytes 776 | tf_op jit(solution)/shard_map/ppermute | solution.py:19
  499.4 18.8 %collective-permute-start.20 = (f32[1,270]{1,0:T(1,128)S(1)}, f32[1,270]{1,0:T(1,128)S(1)}, u32[]{:S(2)}, u32[]{:S(2)}) collective-permute-start(f32[1,270]{1,0:T(1,128)S(1)} %get-tuple-element.32), channel_id=1, source_target_pairs={{32,0},{64,32},{96,64},{128,96},{160,128},{192,160},{224,192},{256... | collective-permute-start | bytes 3248 | tf_op jit(solution)/shard_map/ppermute | solution.py:22
  501.3 16.9 %collective-permute-start.21 = (f32[1,270]{1,0:T(1,128)S(1)}, f32[1,270]{1,0:T(1,128)S(1)}, u32[]{:S(2)}, u32[]{:S(2)}) collective-permute-start(f32[1,270]{1,0:T(1,128)S(1)} %get-tuple-element.33), channel_id=1, source_target_pairs={{0,32},{32,64},{64,96},{96,128},{128,160},{160,192},{192,224},{224... | collective-permute-start | bytes 3248 | tf_op jit(solution)/shard_map/ppermute | solution.py:19
  509.0 4.3 collective-permute-start.16
  510.9 7.3 %collective-permute-start.17 = (f32[64,1]{1,0:T(8,128)S(1)}, f32[64,1]{1,0:T(8,128)S(1)}, u32[]{:S(2)}, u32[]{:S(2)}) collective-permute-start(f32[64,1]{1,0:T(8,128)S(1)} %get-tuple-element.29), channel_id=1, source_target_pairs={{0,1},{1,2},{2,3},{3,4},{4,5},{5,6},{6,7},{7,8},{8,9},{9,10},{10,1... | collective-permute-start | bytes 776 | tf_op jit(solution)/shard_map/ppermute | solution.py:19
  518.4 18.8 %collective-permute-start.22 = (f32[1,270]{1,0:T(1,128)S(1)}, f32[1,270]{1,0:T(1,128)S(1)}, u32[]{:S(2)}, u32[]{:S(2)}) collective-permute-start(f32[1,270]{1,0:T(1,128)S(1)} %get-tuple-element.30), channel_id=1, source_target_pairs={{32,0},{64,32},{96,64},{128,96},{160,128},{192,160},{224,192},{256... | collective-permute-start | bytes 3248 | tf_op jit(solution)/shard_map/ppermute | solution.py:22
  520.3 16.9 %collective-permute-start.23 = (f32[1,270]{1,0:T(1,128)S(1)}, f32[1,270]{1,0:T(1,128)S(1)}, u32[]{:S(2)}, u32[]{:S(2)}) collective-permute-start(f32[1,270]{1,0:T(1,128)S(1)} %get-tuple-element.31), channel_id=1, source_target_pairs={{0,32},{32,64},{64,96},{96,128},{128,160},{160,192},{192,224},{224... | collective-permute-start | bytes 3248 | tf_op jit(solution)/shard_map/ppermute | solution.py:19
  527.9 4.3 collective-permute-start.18
  529.9 7.3 %collective-permute-start.19 = (f32[64,1]{1,0:T(8,128)S(1)}, f32[64,1]{1,0:T(8,128)S(1)}, u32[]{:S(2)}, u32[]{:S(2)}) collective-permute-start(f32[64,1]{1,0:T(8,128)S(1)} %get-tuple-element.27), channel_id=1, source_target_pairs={{0,1},{1,2},{2,3},{3,4},{4,5},{5,6},{6,7},{7,8},{8,9},{9,10},{10,1... | collective-permute-start | bytes 776 | tf_op jit(solution)/shard_map/ppermute | solution.py:19
  537.4 18.8 %collective-permute-start.28 = (f32[1,270]{1,0:T(1,128)S(1)}, f32[1,270]{1,0:T(1,128)S(1)}, u32[]{:S(2)}, u32[]{:S(2)}) collective-permute-start(f32[1,270]{1,0:T(1,128)S(1)} %get-tuple-element.24), channel_id=1, source_target_pairs={{32,0},{64,32},{96,64},{128,96},{160,128},{192,160},{224,192},{256... | collective-permute-start | bytes 3248 | tf_op jit(solution)/shard_map/ppermute | solution.py:22
  539.3 16.9 %collective-permute-start.29 = (f32[1,270]{1,0:T(1,128)S(1)}, f32[1,270]{1,0:T(1,128)S(1)}, u32[]{:S(2)}, u32[]{:S(2)}) collective-permute-start(f32[1,270]{1,0:T(1,128)S(1)} %get-tuple-element.25), channel_id=1, source_target_pairs={{0,32},{32,64},{64,96},{96,128},{128,160},{160,192},{192,224},{224... | collective-permute-start | bytes 3248 | tf_op jit(solution)/shard_map/ppermute | solution.py:19
  548.8 7.3 %collective-permute-start.25 = (f32[64,1]{1,0:T(8,128)S(1)}, f32[64,1]{1,0:T(8,128)S(1)}, u32[]{:S(2)}, u32[]{:S(2)}) collective-permute-start(f32[64,1]{1,0:T(8,128)S(1)} %get-tuple-element.21), channel_id=1, source_target_pairs={{0,1},{1,2},{2,3},{3,4},{4,5},{5,6},{6,7},{7,8},{8,9},{9,10},{10,1... | collective-permute-start | bytes 776 | tf_op jit(solution)/shard_map/ppermute | solution.py:19
  556.4 18.8 %collective-permute-start.30 = (f32[1,270]{1,0:T(1,128)S(1)}, f32[1,270]{1,0:T(1,128)S(1)}, u32[]{:S(2)}, u32[]{:S(2)}) collective-permute-start(f32[1,270]{1,0:T(1,128)S(1)} %get-tuple-element.22), channel_id=1, source_target_pairs={{32,0},{64,32},{96,64},{128,96},{160,128},{192,160},{224,192},{256... | collective-permute-start | bytes 3248 | tf_op jit(solution)/shard_map/ppermute | solution.py:22
  558.3 16.9 %collective-permute-start.31 = (f32[1,270]{1,0:T(1,128)S(1)}, f32[1,270]{1,0:T(1,128)S(1)}, u32[]{:S(2)}, u32[]{:S(2)}) collective-permute-start(f32[1,270]{1,0:T(1,128)S(1)} %get-tuple-element.23), channel_id=1, source_target_pairs={{0,32},{32,64},{64,96},{96,128},{128,160},{160,192},{192,224},{224... | collective-permute-start | bytes 3248 | tf_op jit(solution)/shard_map/ppermute | solution.py:19
  567.8 7.3 %collective-permute-start.27 = (f32[64,1]{1,0:T(8,128)S(1)}, f32[64,1]{1,0:T(8,128)S(1)}, u32[]{:S(2)}, u32[]{:S(2)}) collective-permute-start(f32[64,1]{1,0:T(8,128)S(1)} %get-tuple-element.19), channel_id=1, source_target_pairs={{0,1},{1,2},{2,3},{3,4},{4,5},{5,6},{6,7},{7,8},{8,9},{9,10},{10,1... | collective-permute-start | bytes 776 | tf_op jit(solution)/shard_map/ppermute | solution.py:19
  (11 other events, 1567.2 us)
Sparse Core Ops, SparseCore 0:
  18.0 215.1 all-reduce.2
  236.7 148.0 all-reduce.4
where the time goes:
time: 584 us; the launch traced here: 583 us
  waiting for transfers between devices  404 us (69%)
  starting transfers between devices  110 us (19%)
  blocking collectives  35.5 us (6%)
  between operations  14.6 us (2%)
  other arithmetic  10 us (2%)
  matrix products  6.82 us (1%)
    psum x1, waiting for transfers between devices, shards(): totals = lax.psum(partial_rows, 'lon')  215 us
    psum x1, waiting for transfers between devices, shards(): spectral = lax.psum(partial_value, 'lat') * love_numbers[None, None, :]  149 us
    ppermute x16, starting transfers between devices, extended(): lax.ppermute(lax.slice_in_dim(block, block.shape[dim] - width, None, axis...  79.5 us
    ppermute x16, waiting for transfers between devices, extended(): lax.ppermute(lax.slice_in_dim(block, block.shape[dim] - width, None, axis...  39.4 us
    all_gather x1, blocking collectives, shards(): lax.all_gather(synthesized, 'lon', axis=0, tiled=True)  35.5 us
    ppermute x16, starting transfers between devices, extended(): lax.ppermute(lax.slice_in_dim(block, 0, width, axis=dim), axis, backward)  30.7 us
  transfers between devices with their start and end apart: 34, of which 10 were waited for; matrix products, arithmetic and copies ran while one was open for 0% of the time, Pallas kernels for 0%

commit v1 on v0

--- a/solution.py
+++ b/solution.py
@@ -7,6 +7,11 @@
 SUBSTEPS = 4
 east_step = 0.3
 north_step = 0.3
+
+
+def pipes_spread(peer_axis, local):
+    z2 = lax.all_gather(local, peer_axis).sum(axis=0)
+    return z2
 
 
 def extended(block, sides, width, periodic):
@@ -56,7 +61,7 @@
     owned = lax.dynamic_slice_in_dim(totals, sector_index * (2 * own_waves), 2 * own_waves, 0)
     owned = owned.reshape(own_waves, 2, band_rows)
     partial_value = jnp.einsum("mtl,mpt->mpl", legendre, owned, precision=highest)
-    spectral = lax.psum(partial_value, "lat") * love_numbers[None, None, :]
+    spectral = pipes_spread("lat", partial_value) * love_numbers[None, None, :]
     synthesized = jnp.einsum("mtl,mpl->mpt", legendre, spectral, precision=highest).reshape(
         2 * own_waves, band_rows
     )

time: 584 us -> 519 us (0.89)
  waiting for transfers between devices: 404 us -> 338 us
    psum x1 -> x0, waiting for transfers between devices: 149 us -> none  [shards(): spectral = lax.psum(partial_value, 'lat') * love_numbers[None, None, :]]
    all_gather x0 -> x1, waiting for transfers between devices: none -> 83.5 us  [pipes_spread(): z2 = lax.all_gather(local, peer_axis).sum(axis=0)]
where the time goes in v1:
time: 519 us; the launch traced here: 517 us
  waiting for transfers between devices  338 us (65%)
  starting transfers between devices  110 us (21%)
  blocking collectives  34.6 us (7%)
  between operations  14.6 us (3%)
  other arithmetic  11.7 us (2%)
  matrix products  6 us (1%)
    psum x1, waiting for transfers between devices, shards(): totals = lax.psum(partial_rows, 'lon')  215 us
    all_gather x1, waiting for transfers between devices, pipes_spread(): z2 = lax.all_gather(local, peer_axis).sum(axis=0)  83.5 us
    ppermute x16, starting transfers between devices, extended(): lax.ppermute(lax.slice_in_dim(block, block.shape[dim] - width, None, axis...  78.1 us
    ppermute x16, waiting for transfers between devices, extended(): lax.ppermute(lax.slice_in_dim(block, block.shape[dim] - width, None, axis...  39.4 us
    all_gather x1, blocking collectives, shards(): lax.all_gather(synthesized, 'lon', axis=0, tiled=True)  34.6 us
    ppermute x16, starting transfers between devices, extended(): lax.ppermute(lax.slice_in_dim(block, 0, width, axis=dim), axis, backward)  32.1 us
  transfers between devices with their start and end apart: 34, of which 10 were waited for; matrix products, arithmetic and copies ran while one was open for 0% of the time, Pallas kernels for 0%

profile of v1, /device:TPU:56, one launch (start us, length us, event | category | flops | bytes accessed | tf_op | source)
XLA Modules:
  0.0 517.2 jit_solution(3907386236394708143)
XLA Ops:
  7.2 7.9 %fusion.62 = (f32[128,1,270]{2,1,0:T(1,128)S(1)}, f32[128,1,270]{2,1,0:T(1,128)S(1)}) fusion(s32[270]{0:T(512)S(1)} %iota_add_fusion, s32[128]{0:T(128)} %param.12), kind=kLoop, calls=%fused_computation.98 | loop fusion | flops 311040 | bytes 278072 | tf_op jit(solution)/shard_map/cos | solution.py:36
  15.9 2.0 convolution_multiply_fusion
  18.0 215.3 %all-reduce.2.cloned.1.call-done = f32[256,64]{1,0:T(8,128)} async-done(((f32[256,64]{1,0:T(8,128)}), f32[256,64]{1,0:T(8,128)}) %all-reduce.2.cloned.1.call-update) | async-done | bytes 65552 | tf_op jit(solution)/shard_map/psum | solution.py:60
  235.7 83.5 %all-gather.3.cloned.1.call-done = f32[64,2,2048]{2,1,0:T(2,128)} async-done(((f32[4,2,2048]{2,1,0:T(2,128)}), f32[64,2,2048]{2,1,0:T(2,128)}) %all-gather.3.cloned.1.call-update) | async-done | bytes 1048592 | tf_op jit(solution)/shard_map/all_gather | solution.py:13
  322.7 34.6 %all_gather.11 = f32[256,64]{1,0:T(8,128)S(1)} all-gather(f32[8,64]{1,0:T(8,128)S(1)} %bitcast.11), channel_id=1, replica_groups=mesh['lat'=16,'lon'=32] {'lon'}, dimensions={0}, use_global_device_ids=true | all-gather | bytes 67584 | tf_op jit(solution)/shard_map/all_gather | solution.py:71
  357.9 3.3 collective-permute-start.4
  361.2 6.1 %collective-permute-start.5 = (f32[1,270]{1,0:T(1,128)S(1)}, f32[1,270]{1,0:T(1,128)S(1)}, u32[]{:S(2)}, u32[]{:S(2)}) collective-permute-start(f32[1,270]{1,0:T(1,128)S(1)} %get-tuple-element.49), channel_id=1, source_target_pairs={{0,32},{32,64},{64,96},{96,128},{128,160},{160,192},{192,224},{224... | collective-permute-start | bytes 3248 | tf_op jit(solution)/shard_map/ppermute | solution.py:24
  369.3 2.4 collective-permute-start.1
  371.7 4.9 collective-permute-done.1
  376.9 1.9 collective-permute-start.6
  378.8 7.5 %collective-permute-start.7 = (f32[1,270]{1,0:T(1,128)S(1)}, f32[1,270]{1,0:T(1,128)S(1)}, u32[]{:S(2)}, u32[]{:S(2)}) collective-permute-start(f32[1,270]{1,0:T(1,128)S(1)} %get-tuple-element.47), channel_id=1, source_target_pairs={{0,32},{32,64},{64,96},{96,128},{128,160},{160,192},{192,224},{224... | collective-permute-start | bytes 3248 | tf_op jit(solution)/shard_map/ppermute | solution.py:24
  388.3 2.4 collective-permute-start.3
  390.7 4.9 collective-permute-done.3
  395.8 1.9 collective-permute-start.12
  397.8 7.5 %collective-permute-start.13 = (f32[1,270]{1,0:T(1,128)S(1)}, f32[1,270]{1,0:T(1,128)S(1)}, u32[]{:S(2)}, u32[]{:S(2)}) collective-permute-start(f32[1,270]{1,0:T(1,128)S(1)} %get-tuple-element.41), channel_id=1, source_target_pairs={{0,32},{32,64},{64,96},{96,128},{128,160},{160,192},{192,224},{224... | collective-permute-start | bytes 3248 | tf_op jit(solution)/shard_map/ppermute | solution.py:24
  407.3 2.4 collective-permute-start.9
  409.7 4.9 collective-permute-done.9
  416.7 7.5 %collective-permute-start.15 = (f32[1,270]{1,0:T(1,128)S(1)}, f32[1,270]{1,0:T(1,128)S(1)}, u32[]{:S(2)}, u32[]{:S(2)}) collective-permute-start(f32[1,270]{1,0:T(1,128)S(1)} %get-tuple-element.39), channel_id=1, source_target_pairs={{0,32},{32,64},{64,96},{96,128},{128,160},{160,192},{192,224},{224... | collective-permute-start | bytes 3248 | tf_op jit(solution)/shard_map/ppermute | solution.py:24
  426.3 2.4 collective-permute-start.11
  428.7 4.9 collective-permute-done.11
  435.7 7.5 %collective-permute-start.21 = (f32[1,270]{1,0:T(1,128)S(1)}, f32[1,270]{1,0:T(1,128)S(1)}, u32[]{:S(2)}, u32[]{:S(2)}) collective-permute-start(f32[1,270]{1,0:T(1,128)S(1)} %get-tuple-element.33), channel_id=1, source_target_pairs={{0,32},{32,64},{64,96},{96,128},{128,160},{160,192},{192,224},{224... | collective-permute-start | bytes 3248 | tf_op jit(solution)/shard_map/ppermute | solution.py:24
  445.2 2.4 collective-permute-start.17
  447.7 4.9 collective-permute-done.17
  454.7 7.5 %collective-permute-start.23 = (f32[1,270]{1,0:T(1,128)S(1)}, f32[1,270]{1,0:T(1,128)S(1)}, u32[]{:S(2)}, u32[]{:S(2)}) collective-permute-start(f32[1,270]{1,0:T(1,128)S(1)} %get-tuple-element.31), channel_id=1, source_target_pairs={{0,32},{32,64},{64,96},{96,128},{128,160},{160,192},{192,224},{224... | collective-permute-start | bytes 3248 | tf_op jit(solution)/shard_map/ppermute | solution.py:24
  464.2 2.4 collective-permute-start.19
  466.6 4.9 collective-permute-done.19
  473.6 7.5 %collective-permute-start.29 = (f32[1,270]{1,0:T(1,128)S(1)}, f32[1,270]{1,0:T(1,128)S(1)}, u32[]{:S(2)}, u32[]{:S(2)}) collective-permute-start(f32[1,270]{1,0:T(1,128)S(1)} %get-tuple-element.25), channel_id=1, source_target_pairs={{0,32},{32,64},{64,96},{96,128},{128,160},{160,192},{192,224},{224... | collective-permute-start | bytes 3248 | tf_op jit(solution)/shard_map/ppermute | solution.py:24
  483.2 2.4 collective-permute-start.25
  485.6 4.9 collective-permute-done.25
  492.6 7.5 %collective-permute-start.31 = (f32[1,270]{1,0:T(1,128)S(1)}, f32[1,270]{1,0:T(1,128)S(1)}, u32[]{:S(2)}, u32[]{:S(2)}) collective-permute-start(f32[1,270]{1,0:T(1,128)S(1)} %get-tuple-element.23), channel_id=1, source_target_pairs={{0,32},{32,64},{64,96},{96,128},{128,160},{160,192},{192,224},{224... | collective-permute-start | bytes 3248 | tf_op jit(solution)/shard_map/ppermute | solution.py:24
  502.2 2.4 collective-permute-start.27
  504.6 4.9 collective-permute-done.27
  (91 shorter events, 34.5 us)
Async XLA Ops:
  7.2 226.1 %all-reduce.2.cloned.1.call-start = ((), (), s32[]{:S(2)}) async-start(), calls=%async_computation | async-start | bytes 262144 | tf_op jit(solution)/shard_map/psum | solution.py:60
  17.9 301.3 %all-gather.3.cloned.1.call-start = ((), (), s32[]{:S(2)}) async-start(), calls=%async_computation.1 | async-start | bytes 1114112 | tf_op jit(solution)/shard_map/all_gather | solution.py:13
  357.9 18.8 %collective-permute-start.4 = (f32[1,270]{1,0:T(1,128)S(1)}, f32[1,270]{1,0:T(1,128)S(1)}, u32[]{:S(2)}, u32[]{:S(2)}) collective-permute-start(f32[1,270]{1,0:T(1,128)S(1)} %get-tuple-element.48), channel_id=1, source_target_pairs={{32,0},{64,32},{96,64},{128,96},{160,128},{192,160},{224,192},{256... | collective-permute-start | bytes 3248 | tf_op jit(solution)/shard_map/ppermute | solution.py:27
  361.2 15.5 %collective-permute-start.5 = (f32[1,270]{1,0:T(1,128)S(1)}, f32[1,270]{1,0:T(1,128)S(1)}, u32[]{:S(2)}, u32[]{:S(2)}) collective-permute-start(f32[1,270]{1,0:T(1,128)S(1)} %get-tuple-element.49), channel_id=1, source_target_pairs={{0,32},{32,64},{64,96},{96,128},{128,160},{160,192},{192,224},{224... | collective-permute-start | bytes 3248 | tf_op jit(solution)/shard_map/ppermute | solution.py:24
  367.4 4.3 collective-permute-start
  369.3 7.3 %collective-permute-start.1 = (f32[64,1]{1,0:T(8,128)S(1)}, f32[64,1]{1,0:T(8,128)S(1)}, u32[]{:S(2)}, u32[]{:S(2)}) collective-permute-start(f32[64,1]{1,0:T(8,128)S(1)} %get-tuple-element.45), channel_id=1, source_target_pairs={{0,1},{1,2},{2,3},{3,4},{4,5},{5,6},{6,7},{7,8},{8,9},{9,10},{10,1... | collective-permute-start | bytes 776 | tf_op jit(solution)/shard_map/ppermute | solution.py:24
  376.9 18.8 %collective-permute-start.6 = (f32[1,270]{1,0:T(1,128)S(1)}, f32[1,270]{1,0:T(1,128)S(1)}, u32[]{:S(2)}, u32[]{:S(2)}) collective-permute-start(f32[1,270]{1,0:T(1,128)S(1)} %get-tuple-element.46), channel_id=1, source_target_pairs={{32,0},{64,32},{96,64},{128,96},{160,128},{192,160},{224,192},{256... | collective-permute-start | bytes 3248 | tf_op jit(solution)/shard_map/ppermute | solution.py:27
  378.8 16.9 %collective-permute-start.7 = (f32[1,270]{1,0:T(1,128)S(1)}, f32[1,270]{1,0:T(1,128)S(1)}, u32[]{:S(2)}, u32[]{:S(2)}) collective-permute-start(f32[1,270]{1,0:T(1,128)S(1)} %get-tuple-element.47), channel_id=1, source_target_pairs={{0,32},{32,64},{64,96},{96,128},{128,160},{160,192},{192,224},{224... | collective-permute-start | bytes 3248 | tf_op jit(solution)/shard_map/ppermute | solution.py:24
  386.4 4.3 collective-permute-start.2
  388.3 7.3 %collective-permute-start.3 = (f32[64,1]{1,0:T(8,128)S(1)}, f32[64,1]{1,0:T(8,128)S(1)}, u32[]{:S(2)}, u32[]{:S(2)}) collective-permute-start(f32[64,1]{1,0:T(8,128)S(1)} %get-tuple-element.43), channel_id=1, source_target_pairs={{0,1},{1,2},{2,3},{3,4},{4,5},{5,6},{6,7},{7,8},{8,9},{9,10},{10,1... | collective-permute-start | bytes 776 | tf_op jit(solution)/shard_map/ppermute | solution.py:24
  395.8 18.8 %collective-permute-start.12 = (f32[1,270]{1,0:T(1,128)S(1)}, f32[1,270]{1,0:T(1,128)S(1)}, u32[]{:S(2)}, u32[]{:S(2)}) collective-permute-start(f32[1,270]{1,0:T(1,128)S(1)} %get-tuple-element.40), channel_id=1, source_target_pairs={{32,0},{64,32},{96,64},{128,96},{160,128},{192,160},{224,192},{256... | collective-permute-start | bytes 3248 | tf_op jit(solution)/shard_map/ppermute | solution.py:27
  397.8 16.9 %collective-permute-start.13 = (f32[1,270]{1,0:T(1,128)S(1)}, f32[1,270]{1,0:T(1,128)S(1)}, u32[]{:S(2)}, u32[]{:S(2)}) collective-permute-start(f32[1,270]{1,0:T(1,128)S(1)} %get-tuple-element.41), channel_id=1, source_target_pairs={{0,32},{32,64},{64,96},{96,128},{128,160},{160,192},{192,224},{224... | collective-permute-start | bytes 3248 | tf_op jit(solution)/shard_map/ppermute | solution.py:24
  405.4 4.3 collective-permute-start.8
  407.3 7.3 %collective-permute-start.9 = (f32[64,1]{1,0:T(8,128)S(1)}, f32[64,1]{1,0:T(8,128)S(1)}, u32[]{:S(2)}, u32[]{:S(2)}) collective-permute-start(f32[64,1]{1,0:T(8,128)S(1)} %get-tuple-element.37), channel_id=1, source_target_pairs={{0,1},{1,2},{2,3},{3,4},{4,5},{5,6},{6,7},{7,8},{8,9},{9,10},{10,1... | collective-permute-start | bytes 776 | tf_op jit(solution)/shard_map/ppermute | solution.py:24
  414.8 18.8 %collective-permute-start.14 = (f32[1,270]{1,0:T(1,128)S(1)}, f32[1,270]{1,0:T(1,128)S(1)}, u32[]{:S(2)}, u32[]{:S(2)}) collective-permute-start(f32[1,270]{1,0:T(1,128)S(1)} %get-tuple-element.38), channel_id=1, source_target_pairs={{32,0},{64,32},{96,64},{128,96},{160,128},{192,160},{224,192},{256... | collective-permute-start | bytes 3248 | tf_op jit(solution)/shard_map/ppermute | solution.py:27
  416.7 16.9 %collective-permute-start.15 = (f32[1,270]{1,0:T(1,128)S(1)}, f32[1,270]{1,0:T(1,128)S(1)}, u32[]{:S(2)}, u32[]{:S(2)}) collective-permute-start(f32[1,270]{1,0:T(1,128)S(1)} %get-tuple-element.39), channel_id=1, source_target_pairs={{0,32},{32,64},{64,96},{96,128},{128,160},{160,192},{192,224},{224... | collective-permute-start | bytes 3248 | tf_op jit(solution)/shard_map/ppermute | solution.py:24
  424.3 4.3 collective-permute-start.10
  426.3 7.3 %collective-permute-start.11 = (f32[64,1]{1,0:T(8,128)S(1)}, f32[64,1]{1,0:T(8,128)S(1)}, u32[]{:S(2)}, u32[]{:S(2)}) collective-permute-start(f32[64,1]{1,0:T(8,128)S(1)} %get-tuple-element.35), channel_id=1, source_target_pairs={{0,1},{1,2},{2,3},{3,4},{4,5},{5,6},{6,7},{7,8},{8,9},{9,10},{10,1... | collective-permute-start | bytes 776 | tf_op jit(solution)/shard_map/ppermute | solution.py:24
  433.8 18.8 %collective-permute-start.20 = (f32[1,270]{1,0:T(1,128)S(1)}, f32[1,270]{1,0:T(1,128)S(1)}, u32[]{:S(2)}, u32[]{:S(2)}) collective-permute-start(f32[1,270]{1,0:T(1,128)S(1)} %get-tuple-element.32), channel_id=1, source_target_pairs={{32,0},{64,32},{96,64},{128,96},{160,128},{192,160},{224,192},{256... | collective-permute-start | bytes 3248 | tf_op jit(solution)/shard_map/ppermute | solution.py:27
  435.7 16.9 %collective-permute-start.21 = (f32[1,270]{1,0:T(1,128)S(1)}, f32[1,270]{1,0:T(1,128)S(1)}, u32[]{:S(2)}, u32[]{:S(2)}) collective-permute-start(f32[1,270]{1,0:T(1,128)S(1)} %get-tuple-element.33), channel_id=1, source_target_pairs={{0,32},{32,64},{64,96},{96,128},{128,160},{160,192},{192,224},{224... | collective-permute-start | bytes 3248 | tf_op jit(solution)/shard_map/ppermute | solution.py:24
  443.3 4.3 collective-permute-start.16
  445.2 7.3 %collective-permute-start.17 = (f32[64,1]{1,0:T(8,128)S(1)}, f32[64,1]{1,0:T(8,128)S(1)}, u32[]{:S(2)}, u32[]{:S(2)}) collective-permute-start(f32[64,1]{1,0:T(8,128)S(1)} %get-tuple-element.29), channel_id=1, source_target_pairs={{0,1},{1,2},{2,3},{3,4},{4,5},{5,6},{6,7},{7,8},{8,9},{9,10},{10,1... | collective-permute-start | bytes 776 | tf_op jit(solution)/shard_map/ppermute | solution.py:24
  452.7 18.8 %collective-permute-start.22 = (f32[1,270]{1,0:T(1,128)S(1)}, f32[1,270]{1,0:T(1,128)S(1)}, u32[]{:S(2)}, u32[]{:S(2)}) collective-permute-start(f32[1,270]{1,0:T(1,128)S(1)} %get-tuple-element.30), channel_id=1, source_target_pairs={{32,0},{64,32},{96,64},{128,96},{160,128},{192,160},{224,192},{256... | collective-permute-start | bytes 3248 | tf_op jit(solution)/shard_map/ppermute | solution.py:27
  454.7 16.9 %collective-permute-start.23 = (f32[1,270]{1,0:T(1,128)S(1)}, f32[1,270]{1,0:T(1,128)S(1)}, u32[]{:S(2)}, u32[]{:S(2)}) collective-permute-start(f32[1,270]{1,0:T(1,128)S(1)} %get-tuple-element.31), channel_id=1, source_target_pairs={{0,32},{32,64},{64,96},{96,128},{128,160},{160,192},{192,224},{224... | collective-permute-start | bytes 3248 | tf_op jit(solution)/shard_map/ppermute | solution.py:24
  462.3 4.3 collective-permute-start.18
  464.2 7.3 %collective-permute-start.19 = (f32[64,1]{1,0:T(8,128)S(1)}, f32[64,1]{1,0:T(8,128)S(1)}, u32[]{:S(2)}, u32[]{:S(2)}) collective-permute-start(f32[64,1]{1,0:T(8,128)S(1)} %get-tuple-element.27), channel_id=1, source_target_pairs={{0,1},{1,2},{2,3},{3,4},{4,5},{5,6},{6,7},{7,8},{8,9},{9,10},{10,1... | collective-permute-start | bytes 776 | tf_op jit(solution)/shard_map/ppermute | solution.py:24
  471.7 18.8 %collective-permute-start.28 = (f32[1,270]{1,0:T(1,128)S(1)}, f32[1,270]{1,0:T(1,128)S(1)}, u32[]{:S(2)}, u32[]{:S(2)}) collective-permute-start(f32[1,270]{1,0:T(1,128)S(1)} %get-tuple-element.24), channel_id=1, source_target_pairs={{32,0},{64,32},{96,64},{128,96},{160,128},{192,160},{224,192},{256... | collective-permute-start | bytes 3248 | tf_op jit(solution)/shard_map/ppermute | solution.py:27
  473.6 16.9 %collective-permute-start.29 = (f32[1,270]{1,0:T(1,128)S(1)}, f32[1,270]{1,0:T(1,128)S(1)}, u32[]{:S(2)}, u32[]{:S(2)}) collective-permute-start(f32[1,270]{1,0:T(1,128)S(1)} %get-tuple-element.25), channel_id=1, source_target_pairs={{0,32},{32,64},{64,96},{96,128},{128,160},{160,192},{192,224},{224... | collective-permute-start | bytes 3248 | tf_op jit(solution)/shard_map/ppermute | solution.py:24
  483.2 7.3 %collective-permute-start.25 = (f32[64,1]{1,0:T(8,128)S(1)}, f32[64,1]{1,0:T(8,128)S(1)}, u32[]{:S(2)}, u32[]{:S(2)}) collective-permute-start(f32[64,1]{1,0:T(8,128)S(1)} %get-tuple-element.21), channel_id=1, source_target_pairs={{0,1},{1,2},{2,3},{3,4},{4,5},{5,6},{6,7},{7,8},{8,9},{9,10},{10,1... | collective-permute-start | bytes 776 | tf_op jit(solution)/shard_map/ppermute | solution.py:24
  490.7 18.8 %collective-permute-start.30 = (f32[1,270]{1,0:T(1,128)S(1)}, f32[1,270]{1,0:T(1,128)S(1)}, u32[]{:S(2)}, u32[]{:S(2)}) collective-permute-start(f32[1,270]{1,0:T(1,128)S(1)} %get-tuple-element.22), channel_id=1, source_target_pairs={{32,0},{64,32},{96,64},{128,96},{160,128},{192,160},{224,192},{256... | collective-permute-start | bytes 3248 | tf_op jit(solution)/shard_map/ppermute | solution.py:27
  492.6 16.9 %collective-permute-start.31 = (f32[1,270]{1,0:T(1,128)S(1)}, f32[1,270]{1,0:T(1,128)S(1)}, u32[]{:S(2)}, u32[]{:S(2)}) collective-permute-start(f32[1,270]{1,0:T(1,128)S(1)} %get-tuple-element.23), channel_id=1, source_target_pairs={{0,32},{32,64},{64,96},{96,128},{128,160},{160,192},{192,224},{224... | collective-permute-start | bytes 3248 | tf_op jit(solution)/shard_map/ppermute | solution.py:24
  502.2 7.3 %collective-permute-start.27 = (f32[64,1]{1,0:T(8,128)S(1)}, f32[64,1]{1,0:T(8,128)S(1)}, u32[]{:S(2)}, u32[]{:S(2)}) collective-permute-start(f32[64,1]{1,0:T(8,128)S(1)} %get-tuple-element.19), channel_id=1, source_target_pairs={{0,1},{1,2},{2,3},{3,4},{4,5},{5,6},{6,7},{7,8},{8,9},{9,10},{10,1... | collective-permute-start | bytes 776 | tf_op jit(solution)/shard_map/ppermute | solution.py:24
  (11 other events, 987.7 us)
Sparse Core Ops, SparseCore 0:
  18.0 215.1 all-reduce.1
  237.0 82.1 all-gather.2
